TPU v7x, 32 devices: a whole 2x2x4 slice. The times are simulated.
32 devices in a mesh: fsdp: 4 (over y, x), heads: 2 (over core), tensor: 4 (over z).
Axes of the slice: x: 2, y: 2, z: 4, core: 2. Of those that a mesh axis runs over, the one named last changes fastest.
Arguments:
- inputs: float32 [32, 729, 1152], P(('fsdp', 'heads', 'tensor')), may hold values from -6 to 6
- cotangent: float32 [32, 729, 1152], P(('fsdp', 'heads', 'tensor')), may hold values from -6 to 6
- image_adapter_index: int32 [32], replicated, may hold values from 0 to 7
- first_norm_gain: float32 [1152], replicated, may hold values from 0.5 to 1.5
- first_norm_bias: float32 [1152], replicated, may hold values from -3 to 3
- second_norm_gain: float32 [1152], replicated, may hold values from 0.5 to 1.5
- second_norm_bias: float32 [1152], replicated, may hold values from -3 to 3
- query_key_value_weight: bfloat16 [1152, 3, 1152], P('fsdp', None, 'heads'), may hold values from -0.1875 to 0.1875
- attention_output_weight: bfloat16 [1152, 1152], P('fsdp', 'heads'), may hold values from -3 to 3
- up_weight: bfloat16 [1152, 4304], P('fsdp', 'tensor'), may hold values from -0.1875 to 0.1875
- down_weight: bfloat16 [1152, 4304], P('fsdp', 'tensor'), may hold values from -0.09375 to 0.09375
- up_projection_bias: bfloat16 [4304], P('tensor'), may hold values from -3 to 3
- down_projection_bias: bfloat16 [1152], replicated, may hold values from -3 to 3
- query_key_value_adapter_first: bfloat16 [3, 8, 1152, 16], replicated, may hold values from -0.1875 to 0.1875
- query_key_value_adapter_second: bfloat16 [3, 8, 16, 1152], P(None, None, None, 'heads'), may hold values from -0.75 to 0.75
- projection_adapter_first: bfloat16 [8, 1152, 16], P(None, 'heads'), may hold values from -3 to 3
- projection_adapter_second: bfloat16 [8, 16, 1152], replicated, may hold values from -0.75 to 0.75
- up_adapter_first: bfloat16 [8, 1152, 16], replicated, may hold values from -0.1875 to 0.1875
- up_adapter_second: bfloat16 [8, 16, 4304], P(None, None, 'tensor'), may hold values from -0.75 to 0.75
- down_adapter_first: bfloat16 [8, 16, 4304], P(None, None, 'tensor'), may hold values from -0.09375 to 0.09375
- down_adapter_second: bfloat16 [8, 16, 1152], replicated, may hold values from -0.75 to 0.75
Outputs:
- layer_output: float32 [32, 729, 1152], P(('fsdp', 'heads', 'tensor'))
- grad_input: float32 [32, 729, 1152], P(('fsdp', 'heads', 'tensor'))
- grad_qkv_in: float32 [3, 8, 1152, 16], replicated
- grad_qkv_out: float32 [3, 8, 16, 1152], P(None, None, None, 'heads')
- grad_proj_in: float32 [8, 1152, 16], P(None, 'heads')
- grad_proj_out: float32 [8, 16, 1152], replicated
- grad_up_in: float32 [8, 1152, 16], replicated
- grad_up_out: float32 [8, 16, 4304], P(None, None, 'tensor')
- grad_down_in: float32 [8, 16, 4304], P(None, None, 'tensor')
- grad_down_out: float32 [8, 16, 1152], replicated
All inputs are finite; a program needn't handle non-finite values.
Results may differ from a plain program's by a relative error of at most 0.02.
Values may be sent and summed in bfloat16 or wider, within the bound.
A program may use at most 256 MiB of HBM per device.

v0:
```python
import jax
import jax.numpy as jnp
from jax import lax
from jax.sharding import PartitionSpec as P

HEAD_DIM = 72


highest_precision = lax.Precision.HIGHEST
norm_eps = 1e-06


def normalize(values, gain, bias):
    mean = jnp.mean(values, axis=-1, keepdims=True)
    centred = values - mean
    inverse = lax.rsqrt(jnp.mean(centred * centred, axis=-1, keepdims=True) + norm_eps)
    unit = centred * inverse
    return (unit * gain + bias, unit, inverse)


def normalize_back(grad_norm, unit, inverse, gain):
    scaled = grad_norm * gain
    return inverse * (
        scaled
        - jnp.mean(scaled, axis=-1, keepdims=True)
        - unit * jnp.mean(scaled * unit, axis=-1, keepdims=True)
    )


def gelu_tanh(values):
    return jax.nn.gelu(values, approximate=True)


def one_hot(ids, count):
    return (ids[:, None] == jnp.arange(count, dtype=jnp.int32)[None, :]).astype(jnp.float32)


def by_adapter(hot, per_image):
    return jnp.einsum("ia,ixy->axy", hot, per_image, precision=highest_precision)


def attend_forward(operands):
    query, keyed, valued = operands
    scores = jnp.einsum(
        "qhd,khd->hqk", query, keyed, preferred_element_type=jnp.float32
    ) * HEAD_DIM ** (-0.5)
    top = jnp.max(scores, axis=-1, keepdims=True)
    weights = jnp.exp(scores - top)
    total = jnp.sum(weights, axis=-1, keepdims=True)
    probs = (weights / total).astype(jnp.bfloat16)
    mixed_heads = jnp.einsum("hqk,khd->qhd", probs, valued, preferred_element_type=jnp.float32)
    return (mixed_heads.astype(jnp.bfloat16), (top + jnp.log(total))[..., 0])


def attend_back(operands):
    query, keyed, valued, grad_mixed, log_total = operands
    scale = HEAD_DIM ** (-0.5)
    scores = jnp.einsum("qhd,khd->hqk", query, keyed, preferred_element_type=jnp.float32) * scale
    probs = jnp.exp(scores - log_total[..., None])
    grad_probs = jnp.einsum("qhd,khd->hqk", grad_mixed, valued, preferred_element_type=jnp.float32)
    grad_values = jnp.einsum(
        "hqk,qhd->khd", probs.astype(jnp.bfloat16), grad_mixed, preferred_element_type=jnp.float32
    )
    inner = jnp.sum(probs * grad_probs, axis=-1, keepdims=True)
    grad_scores = (probs * (grad_probs - inner)).astype(jnp.bfloat16)
    grad_query = (
        jnp.einsum("hqk,khd->qhd", grad_scores, keyed, preferred_element_type=jnp.float32) * scale
    )
    grad_keys = (
        jnp.einsum("hqk,qhd->khd", grad_scores, query, preferred_element_type=jnp.float32) * scale
    )
    return (grad_query, grad_keys, grad_values)


def per_device(
    inputs,
    cotangent,
    image_adapter_index,
    first_norm_gain,
    first_norm_bias,
    second_norm_gain,
    second_norm_bias,
    query_key_value_weight,
    attention_output_weight,
    up_weight,
    down_weight,
    up_projection_bias,
    down_projection_bias,
    query_key_value_adapter_first,
    query_key_value_adapter_second,
    projection_adapter_first,
    projection_adapter_second,
    up_adapter_first,
    up_adapter_second,
    down_adapter_first,
    down_adapter_second,
):
    head_count = lax.axis_size("heads")
    unit_count = lax.axis_size("tensor")
    fsdp_index = lax.axis_index("fsdp")
    head_index = lax.axis_index("heads")
    unit_index = lax.axis_index("tensor")
    images, length, width = inputs.shape
    adapter_factors = query_key_value_adapter_first.shape[1]
    local = jnp.arange(images, dtype=jnp.int32)
    group = fsdp_index * head_count
    own_rows = ((group + head_index) * unit_count + unit_index) * images + local
    head_rows = (
        ((group + jnp.arange(head_count, dtype=jnp.int32))[:, None] * unit_count + unit_index)
        * images
        + local[None, :]
    ).reshape(-1)
    unit_rows = (
        ((group + head_index) * unit_count + jnp.arange(unit_count, dtype=jnp.int32))[:, None]
        * images
        + local[None, :]
    ).reshape(-1)
    owned_numbers = image_adapter_index[own_rows]
    head_numbers = image_adapter_index[head_rows]
    unit_numbers = image_adapter_index[unit_rows]
    query_key_value_whole, output_whole_weight, up_rows, down_rows = (
        lax.all_gather(query_key_value_weight, "fsdp", axis=0, tiled=True),
        lax.all_gather(attention_output_weight, "fsdp", axis=0, tiled=True),
        lax.all_gather(up_weight, "fsdp", axis=0, tiled=True),
        lax.all_gather(down_weight, "fsdp", axis=0, tiled=True),
    )
    norm1, unit1, inverse1 = normalize(inputs, first_norm_gain, first_norm_bias)
    ln1_all = lax.all_gather(norm1.astype(jnp.bfloat16), "heads", axis=0, tiled=True)
    (
        query_key_value_attention,
        output_attention_part,
        query_key_value_output_weight,
        projection_input_weight,
    ) = (
        query_key_value_whole,
        output_whole_weight,
        query_key_value_adapter_second,
        projection_adapter_first,
    )
    seen = ln1_all.shape[0]
    query_key_value_input_selected = query_key_value_adapter_first[:, head_numbers]
    qkv_out_sel = query_key_value_output_weight[:, head_numbers]
    query_key_value_middle = jnp.einsum(
        "obl,holm->hobm",
        ln1_all,
        query_key_value_input_selected,
        preferred_element_type=jnp.float32,
    )
    projected = jnp.einsum(
        "isd,djf->jisf", ln1_all, query_key_value_attention, preferred_element_type=jnp.float32
    )
    projected = projected + jnp.einsum(
        "klty,klye->klte",
        query_key_value_middle,
        qkv_out_sel.astype(jnp.float32),
        precision=highest_precision,
    )
    proj_low = projected.astype(jnp.bfloat16)
    local_width = proj_low.shape[-1]
    heads_local = local_width // HEAD_DIM
    shaped = proj_low.reshape(3, seen, length, heads_local, HEAD_DIM)
    mixed_heads, log_total = lax.map(attend_forward, (shaped[0], shaped[1], shaped[2]))
    mixed_heads = mixed_heads.reshape(seen, length, local_width)
    proj_in_sel = projection_input_weight[head_numbers]
    projection_output_selected = projection_adapter_second[head_numbers]
    projection_adapter_middle = jnp.einsum(
        "lby,lyg->lbg", mixed_heads, proj_in_sel, preferred_element_type=jnp.float32
    )
    attention_branch = jnp.einsum(
        "ise,de->isd", mixed_heads, output_attention_part, preferred_element_type=jnp.float32
    )
    attention_branch = attention_branch + jnp.einsum(
        "cmt,ctf->cmf",
        projection_adapter_middle,
        projection_output_selected.astype(jnp.float32),
        precision=highest_precision,
    )
    hidden = inputs + lax.psum_scatter(
        attention_branch.astype(jnp.bfloat16), "heads", scatter_dimension=0, tiled=True
    ).astype(jnp.float32)
    norm2, unit2, inverse2 = normalize(hidden, second_norm_gain, second_norm_bias)
    second_norm_reduced = norm2.astype(jnp.bfloat16)
    up_adapter_middle = jnp.einsum(
        "ego,eoh->egh",
        second_norm_reduced,
        up_adapter_first[owned_numbers],
        preferred_element_type=jnp.float32,
    ).astype(jnp.bfloat16)
    ln2_in, up_mid_in = (
        lax.all_gather(second_norm_reduced, "tensor", axis=0, tiled=True),
        lax.all_gather(up_adapter_middle, "tensor", axis=0, tiled=True),
    )
    up_cols, down_cols, bias_cols = (up_rows, down_rows, up_projection_bias)
    up_output_columns, down_input_columns = (up_adapter_second, down_adapter_first)
    up_input_selected = up_adapter_first[unit_numbers]
    up_out_sel = up_output_columns[unit_numbers]
    down_in_sel = down_input_columns[unit_numbers]
    down_output_selected = down_adapter_second[unit_numbers]
    residual_before = jnp.einsum(
        "isd,df->isf", ln2_in, up_cols, preferred_element_type=jnp.float32
    ) + bias_cols.astype(jnp.float32)
    residual_before = residual_before + jnp.einsum(
        "cbd,cdp->cbp",
        up_mid_in.astype(jnp.float32),
        up_out_sel.astype(jnp.float32),
        precision=highest_precision,
    )
    act_low = gelu_tanh(residual_before).astype(jnp.bfloat16)
    down_adapter_middle = jnp.einsum(
        "pco,pqo->pcq", act_low, down_in_sel, preferred_element_type=jnp.float32
    )
    mlp_part = jnp.einsum("isf,df->isd", act_low, down_cols, preferred_element_type=jnp.float32)
    mlp_part = mlp_part + jnp.einsum(
        "cmt,ctf->cmf",
        down_adapter_middle,
        down_output_selected.astype(jnp.float32),
        precision=highest_precision,
    )
    mlp_sum = lax.psum_scatter(
        mlp_part.astype(jnp.bfloat16), "tensor", scatter_dimension=0, tiled=True
    ).astype(jnp.float32)
    layer_output = hidden + mlp_sum + down_projection_bias.astype(jnp.float32)
    grad_mlp = cotangent.astype(jnp.bfloat16)
    grad_mlp_in = lax.all_gather(grad_mlp, "tensor", axis=0, tiled=True)
    grad_down_mid = jnp.einsum(
        "isd,ird->isr", grad_mlp_in, down_output_selected, preferred_element_type=jnp.float32
    )
    grad_act = jnp.einsum("isd,df->isf", grad_mlp_in, down_cols, preferred_element_type=jnp.float32)
    grad_act = grad_act + jnp.einsum(
        "cbd,cdp->cbp", grad_down_mid, down_in_sel.astype(jnp.float32), precision=highest_precision
    )
    ignored, gelu_pull = jax.vjp(gelu_tanh, residual_before)
    grad_before = gelu_pull(grad_act)[0].astype(jnp.bfloat16)
    grad_up_mid = jnp.einsum(
        "pco,pqo->pcq", grad_before, up_out_sel, preferred_element_type=jnp.float32
    )
    grad_ln2 = jnp.einsum("isf,df->isd", grad_before, up_cols, preferred_element_type=jnp.float32)
    grad_ln2 = grad_ln2 + jnp.einsum(
        "isr,idr->isd",
        grad_up_mid,
        up_input_selected.astype(jnp.float32),
        precision=highest_precision,
    )
    grad_ln2 = lax.psum_scatter(
        grad_ln2.astype(jnp.bfloat16), "tensor", scatter_dimension=0, tiled=True
    ).astype(jnp.float32)
    grad_hidden = cotangent + normalize_back(grad_ln2, unit2, inverse2, second_norm_gain)
    mlp_hot = one_hot(unit_numbers, adapter_factors)
    grad_up_in_part = by_adapter(
        mlp_hot, jnp.einsum("isd,isr->idr", ln2_in, grad_up_mid, precision=highest_precision)
    )
    grad_up_out_part = by_adapter(
        mlp_hot,
        jnp.einsum("isr,isf->irf", up_mid_in, grad_before, preferred_element_type=jnp.float32),
    )
    grad_down_in_part = by_adapter(
        mlp_hot, jnp.einsum("isr,isf->irf", grad_down_mid, act_low, precision=highest_precision)
    )
    grad_down_out_part = by_adapter(
        mlp_hot,
        jnp.einsum("isr,isd->ird", down_adapter_middle, grad_mlp_in, precision=highest_precision),
    )
    grad_branch = lax.all_gather(grad_hidden.astype(jnp.bfloat16), "heads", axis=0, tiled=True)
    grad_proj_mid = jnp.einsum(
        "isd,ird->isr", grad_branch, projection_output_selected, preferred_element_type=jnp.float32
    )
    grad_mixed = jnp.einsum(
        "isd,de->ise", grad_branch, output_attention_part, preferred_element_type=jnp.float32
    )
    grad_mixed = grad_mixed + jnp.einsum(
        "isr,ier->ise", grad_proj_mid, proj_in_sel.astype(jnp.float32), precision=highest_precision
    )
    grad_mixed = grad_mixed.astype(jnp.bfloat16).reshape(seen, length, heads_local, HEAD_DIM)
    grad_query, grad_keys, grad_values = lax.map(
        attend_back, (shaped[0], shaped[1], shaped[2], grad_mixed, log_total)
    )
    grad_proj = (
        jnp.stack([grad_query, grad_keys, grad_values])
        .reshape(3, seen, length, local_width)
        .astype(jnp.bfloat16)
    )
    grad_qkv_mid = jnp.einsum(
        "jisf,jirf->jisr", grad_proj, qkv_out_sel, preferred_element_type=jnp.float32
    )
    grad_ln1 = jnp.einsum(
        "jisf,djf->isd", grad_proj, query_key_value_attention, preferred_element_type=jnp.float32
    )
    grad_ln1 = grad_ln1 + jnp.einsum(
        "jisr,jidr->isd",
        grad_qkv_mid,
        query_key_value_input_selected.astype(jnp.float32),
        precision=highest_precision,
    )
    grad_ln1 = lax.psum_scatter(
        grad_ln1.astype(jnp.bfloat16), "heads", scatter_dimension=0, tiled=True
    ).astype(jnp.float32)
    grad_input = grad_hidden + normalize_back(grad_ln1, unit1, inverse1, first_norm_gain)
    attn_hot = one_hot(head_numbers, adapter_factors)
    qkv_in_image = jnp.einsum("isd,jisr->jidr", ln1_all, grad_qkv_mid, precision=highest_precision)
    grad_qkv_in_part = jnp.einsum(
        "ia,jidr->jadr", attn_hot, qkv_in_image, precision=highest_precision
    )
    qkv_out_image = jnp.einsum(
        "jisr,jisf->jirf", query_key_value_middle, grad_proj, precision=highest_precision
    )
    grad_qkv_out_part = jnp.einsum(
        "ia,jirf->jarf", attn_hot, qkv_out_image, precision=highest_precision
    )
    grad_proj_in_part = by_adapter(
        attn_hot,
        jnp.einsum("ise,isr->ier", mixed_heads, grad_proj_mid, precision=highest_precision),
    )
    grad_proj_out_part = by_adapter(
        attn_hot,
        jnp.einsum(
            "isr,isd->ird", projection_adapter_middle, grad_branch, precision=highest_precision
        ),
    )
    grad_qkv_in, grad_proj_out, grad_up_in, grad_down_out = lax.psum(
        (grad_qkv_in_part, grad_proj_out_part, grad_up_in_part, grad_down_out_part),
        ("fsdp", "heads", "tensor"),
    )
    grad_qkv_out, grad_proj_in = lax.psum(
        (grad_qkv_out_part, grad_proj_in_part), ("fsdp", "tensor")
    )
    grad_up_out, grad_down_in = (
        lax.psum(grad_up_out_part.astype(jnp.bfloat16), ("fsdp", "heads")).astype(jnp.float32),
        lax.psum(grad_down_in_part.astype(jnp.bfloat16), ("fsdp", "heads")).astype(jnp.float32),
    )
    return (
        layer_output,
        grad_input,
        grad_qkv_in,
        grad_qkv_out,
        grad_proj_in,
        grad_proj_out,
        grad_up_in,
        grad_up_out,
        grad_down_in,
        grad_down_out,
    )


def solution(mesh):
    in_specs = (
        P(("fsdp", "heads", "tensor"), None, None),
        P(("fsdp", "heads", "tensor"), None, None),
        P(),
        P(),
        P(),
        P(),
        P(),
        P("fsdp", None, "heads"),
        P("fsdp", "heads"),
        P("fsdp", "tensor"),
        P("fsdp", "tensor"),
        P("tensor"),
        P(),
        P(),
        P(None, None, None, "heads"),
        P(None, "heads", None),
        P(),
        P(),
        P(None, None, "tensor"),
        P(None, None, "tensor"),
        P(),
    )
    out_specs = (
        P(("fsdp", "heads", "tensor"), None, None),
        P(("fsdp", "heads", "tensor"), None, None),
        P(),
        P(None, None, None, "heads"),
        P(None, "heads", None),
        P(),
        P(),
        P(None, None, "tensor"),
        P(None, None, "tensor"),
        P(),
    )
    return jax.shard_map(
        per_device, mesh=mesh, in_specs=in_specs, out_specs=out_specs, check_vma=False
    )
```

profile of v0, /device:TPU:0, one launch (start us, length us, event | category | flops | bytes accessed | tf_op | source)
XLA Modules:
  0.0 1267.5 jit_solution(7760785568148674721)
XLA Ops:
  36.3 54.6 %all-gather.13.cloned.1.call-done = bf16[1152,3,576]{2,0,1:T(8,128)(2,1)} async-done(((bf16[288,3,576]{2,0,1:T(8,128)(2,1)}), bf16[1152,3,576]{2,0,1:T(8,128)(2,1)}) %all-gather.13.cloned.1.call-update) | async-done | bytes 3981328 | tf_op jit(solution)/shard_map/all_gather | solution.py:122
  90.9 10.7 fusion.59
  109.1 57.2 %while.28 = (s32[]{:T(128)}, bf16[2,729,8,72]{1,3,2,0:T(8,128)(2,1)}, f32[2,8,729]{2,1,0:T(8,128)S(1)}, bf16[2,729,8,72]{1,3,2,0:T(8,128)(2,1)}, bf16[2,729,8,72...) while((s32[]{:T(128)}, bf16[2,729,8,72]{1,3,2,0:T(8,128)(2,1)}, ...), condition=%wide.region_5.6_spmd, body=%wide.region_2.5_spmd.sunk | while | flops 1263117824 | bytes 55831608 | solution.py:162
  202.4 102.8 %all-gather.23.cloned.1.call-done = bf16[4,729,1152]{2,1,0:T(8,128)(2,1)} async-done(((bf16[1,729,1152]{2,1,0:T(8,128)(2,1)}), bf16[4,729,1152]{2,1,0:T(8,128)(2,1)}) %all-gather.23.cloned.1.call-update) | async-done | bytes 6718480 | tf_op jit(solution)/shard_map/all_gather | solution.py:224
  310.0 34.9 %all-gather.21.cloned.1.call-done = bf16[1152,1076]{1,0:T(8,128)(2,1)} async-done(((bf16[288,1076]{1,0:T(8,128)(2,1)}), bf16[1152,1076]{1,0:T(8,128)(2,1)}) %all-gather.21.cloned.1.call-update) | async-done | bytes 2479120 | tf_op jit(solution)/shard_map/all_gather | solution.py:125
  344.9 14.5 %fusion.69 = f32[4,729,1076]{1,2,0:T(8,128)} fusion(bf16[4,729,1152]{2,1,0:T(8,128)(2,1)} %all-gather.23.cloned.1.call-done, bf16[1152,1076]{1,0:T(8,128)(2,1)} %all-gather.21.cloned.1.call-done), kind=kOutput, calls=%fused_computation.114 | convolution fusion | flops 7229067264 | bytes 21748032 | tf_op jit(solution)/shard_map/isd,df->isf/dot_general | solution.py:228
  359.9 13.4 %all-gather.1 = bf16[4,729,16]{1,2,0:T(8,128)(2,1)S(1)} all-gather(bf16[1,729,16]{1,2,0:T(8,128)(2,1)S(1)} %fusion.92), channel_id=2, replica_groups=mesh['fsdp'=4,'heads'=2,'tensor'=4] {'tensor'}, dimensions={0}, use_global_device_ids=true | all-gather | bytes 116640 | tf_op jit(solution)/shard_map/all_gather | solution.py:191
  373.3 13.0 %all-gather.19.cloned.1.call-done = bf16[1152,1076]{1,0:T(8,128)(2,1)} async-done(((bf16[288,1076]{1,0:T(8,128)(2,1)}), bf16[1152,1076]{1,0:T(8,128)(2,1)}) %all-gather.19.cloned.1.call-update) | async-done | bytes 2479120 | tf_op jit(solution)/shard_map/all_gather | solution.py:124
  386.4 124.8 %all-gather.17.cloned.1.call-done = bf16[4,729,1152]{2,1,0:T(8,128)(2,1)} async-done(((bf16[1,729,1152]{2,1,0:T(8,128)(2,1)}), bf16[4,729,1152]{2,1,0:T(8,128)(2,1)}) %all-gather.17.cloned.1.call-update) | async-done | bytes 6718480 | tf_op jit(solution)/shard_map/all_gather | solution.py:190
  511.2 12.4 fusion.75
  533.7 18.5 %fusion.50 = bf16[4,729,1076]{1,2,0:T(8,128)(2,1)S(1)} fusion(f32[4,729,1076]{1,2,0:T(8,128)} %get-tuple-element.204, f32[4,729,1076]{1,2,0:T(8,128)} %fusion.69, f32[4,16,729]{2,1,0:T(8,128)S(1)} %fusion.138, bf16[4,16,1076]{2,1,0:T(8,128)(2,1)S(1)} %gather_fusion.7), kind=kOutput, calls=%fused_computation.72 | convolution fusion | flops 668312192 | bytes 31700512 | tf_op jit(solution)/shard_map/cbd,cdp->cbp/dot_general | solution.py:229
  555.9 13.1 %fusion.73 = f32[4,729,1152]{2,1,0:T(8,128)} fusion(bf16[4,729,1076]{1,2,0:T(8,128)(2,1)S(1)} %fusion.50, bf16[1152,1076]{1,0:T(8,128)(2,1)S(1)} %copy-done.56), kind=kOutput, calls=%fused_computation.118 | convolution fusion | flops 7229067264 | bytes 22191264 | tf_op jit(solution)/shard_map/isf,df->isd/dot_general | solution.py:237
  569.0 10.8 add_convert_fusion
  583.9 13.5 %fusion.71 = f32[4,729,1152]{2,1,0:T(8,128)S(1)} fusion(bf16[4,729,1076]{1,2,0:T(8,128)(2,1)} %get-tuple-element.203, bf16[1152,1076]{1,0:T(8,128)(2,1)S(1)} %copy-done.55), kind=kOutput, calls=%fused_computation.116 | convolution fusion | flops 7229067264 | bytes 22191264 | tf_op jit(solution)/shard_map/isf,df->isd/dot_general | solution.py:212
  606.6 90.2 %reduce-scatter.9.cloned.1.call-done = bf16[1,729,1152]{2,1,0:T(8,128)(2,1)} async-done(((bf16[4,729,1152]{2,1,0:T(8,128)(2,1)}), bf16[1,729,1152]{2,1,0:T(8,128)(2,1)}) %reduce-scatter.9.cloned.1.call-update) | async-done | bytes 1679632 | tf_op jit(solution)/shard_map/reduce_scatter | solution.py:244
  700.4 118.0 %reduce-scatter.7.cloned.1.call-done = bf16[1,729,1152]{2,1,0:T(8,128)(2,1)} async-done(((bf16[4,729,1152]{2,1,0:T(8,128)(2,1)}), bf16[1,729,1152]{2,1,0:T(8,128)(2,1)}) %reduce-scatter.7.cloned.1.call-update) | async-done | bytes 1679632 | tf_op jit(solution)/shard_map/reduce_scatter | solution.py:219
  863.4 99.9 %while.29 = (s32[]{:T(128)}, bf16[2,729,8,72]{1,3,2,0:T(8,128)(2,1)}, bf16[2,729,8,72]{1,3,2,0:T(8,128)(2,1)}, bf16[2,729,8,72]{1,3,2,0:T(8,128)(2,1)}, bf16[2,7...) while((s32[]{:T(128)}, ...), condition=%wide.region_15.16_spmd, body=%wide.region_13.15_spmd.sunk | while | flops 3112952320 | bytes 200497152 | solution.py:274
  882.1 12.7 %multiply_reduce_fusion.9 = (f32[8,729]{1,0:T(8,128)S(1)}, f32[8,729,729]{1,2,0:T(8,128)}) fusion(f32[8,729,729]{1,2,0:T(8,128)} %fusion.216, f32[8,729]{1,0:T(8,128)S(1)} %dynamic-slice_bitcast_fusion.2, bf16[2,729,8,72]{1,3,2,0:T(8,128)(2,1)S(1)} %copy-done.13, s32[]{:T(128)S(6)} %copy.187, bf16[2,729,8,72]{1,3,2,0:T(8,128)(2,1)S(1)} %copy-done.9), kind=kOutput, calls=%fused_computation.30.clone.1 | convolution fusion | flops 629220288 | bytes 35830624 | tf_op jit(solution)/shard_map/while/body/eval_jaxpr/qhd,khd->hqk/dot_general | solution.py:60
  894.8 13.2 %multiply_convert_fusion.3 = bf16[8,729,729]{1,2,0:T(8,128)(2,1)S(1)} fusion(f32[8,729,729]{1,2,0:T(8,128)} %get-tuple-element.305, f32[8,729,729]{1,2,0:T(8,128)} %fusion.216, f32[8,729]{1,0:T(8,128)S(1)} %get-tuple-element.306, f32[8,729]{1,0:T(8,128)S(1)} %dynamic-slice_bitcast_fusion.2), kind=kLoop, calls=%fused_computation.29.clone.1 | loop fusion | flops 21257640 | bytes 42561936 | tf_op jit(solution)/shard_map/while/body/eval_jaxpr/convert_element_type | solution.py:65
  932.0 12.6 multiply_reduce_fusion.9
  944.5 13.1 %multiply_convert_fusion.3 = bf16[8,729,729]{1,2,0:T(8,128)(2,1)S(1)} fusion(f32[8,729,729]{1,2,0:T(8,128)} %get-tuple-element.305, f32[8,729,729]{1,2,0:T(8,128)} %fusion.216, f32[8,729]{1,0:T(8,128)S(1)} %get-tuple-element.306, f32[8,729]{1,0:T(8,128)S(1)} %dynamic-slice_bitcast_fusion.2), kind=kLoop, calls=%fused_computation.29.clone.1 | loop fusion | flops 21257640 | bytes 42561936 | tf_op jit(solution)/shard_map/while/body/eval_jaxpr/convert_element_type | solution.py:65
  983.7 11.9 fusion.57
  1011.3 76.5 %all-reduce.9.cloned.1.call-done = (f32[3,8,16,576]{3,1,2,0:T(8,128)}, f32[8,576,16]{1,0,2:T(8,128)}) async-done(((f32[3,8,16,576]{3,1,2,0:T(8,128)}, f32[8,576,16]{1,0,2:T(8,128)}), (f32[3,8,16,576]{3,1,2,0:T(8,128)}, f32[8,576,16]{1,0,2:T(8,128)})) %all-reduce.9.cloned.1.call-update) | async-done | bytes 1179664 | tf_op jit(solution)/shard_map/psum | solution.py:323
  1091.8 142.8 %all-reduce.7.cloned.1.call-done = (f32[3,8,1152,16]{2,1,3,0:T(8,128)}, f32[8,16,1152]{2,0,1:T(8,128)}, f32[8,1152,16]{1,0,2:T(8,128)}, f32[8,16,1152]{2,0,1:T(8,128)}) async-done(((f32[3,8,1152,16]{2,1,3,0:T(8,128)}, f32[8,16,1152]{2,0,1:T(8,128)}, f32[8,1152,16]{1,0,2:T(8,128)}, f32[8,16,1152]{2,0,1:T(8,128)}), (f32[3,8,1152,16]{2,1,3,0:T(8,128)}, f32[8,16,1152]{2,0,1:T(8,128)}, f32[8,1152,16]{1,0,2:T(8,128)}, ...) | async-done | bytes 3538960 | tf_op jit(solution)/shard_map/psum | solution.py:319
  (296 shorter events, 320.1 us)
Async XLA Ops:
  8.0 17.2 %copy-start = (bf16[3,8,1152,16]{2,3,1,0:T(8,128)(2,1)S(1)}, bf16[3,8,1152,16]{2,3,1,0:T(8,128)(2,1)}, u32[]{:S(2)}) copy-start(bf16[3,8,1152,16]{2,3,1,0:T(8,128)(2,1)} %param.38) | copy-start | bytes 2654212
  8.0 25.2 %all-gather.11.cloned.1.call-start = ((), (), s32[]{:S(2)}) async-start(), calls=%async_computation.4 | async-start | bytes 5087232 | tf_op jit(solution)/shard_map/all_gather | solution.py:128
  17.9 73.0 %all-gather.13.cloned.1.call-start = ((), (), s32[]{:S(2)}) async-start(), calls=%async_computation.5 | async-start | bytes 5529600 | tf_op jit(solution)/shard_map/all_gather | solution.py:122
  18.6 150.3 %all-gather.15.cloned.1.call-start = ((), (), s32[]{:S(2)}) async-start(), calls=%async_computation.6 | async-start | bytes 1843200 | tf_op jit(solution)/shard_map/all_gather | solution.py:123
  19.4 170.4 %reduce-scatter.5.cloned.1.call-start = ((), (), s32[]{:S(2)}) async-start(), calls=%async_computation.7 | async-start | bytes 5087232 | tf_op jit(solution)/shard_map/reduce_scatter | solution.py:178
  25.2 76.4 %copy-start.32 = (bf16[2,3,16,576]{3,2,1,0:T(8,128)(2,1)}, bf16[2,3,16,576]{3,2,1,0:T(8,128)(2,1)S(1)}, u32[]{:S(2)}) copy-start(bf16[2,3,16,576]{3,2,1,0:T(8,128)(2,1)S(1)} %gather_fusion.2) | copy-start | bytes 331780
  25.8 75.8 %copy-start.11 = (bf16[2,3,1152,16]{2,3,1,0:T(8,128)(2,1)}, bf16[2,3,1152,16]{2,3,1,0:T(8,128)(2,1)S(1)}, u32[]{:S(2)}) copy-start(bf16[2,3,1152,16]{2,3,1,0:T(8,128)(2,1)S(1)} %gather_fusion.1) | copy-start | bytes 663556
  36.3 65.4 %copy-start.25 = (f32[3,2,729,16]{2,3,0,1:T(8,128)}, f32[3,2,729,16]{2,3,0,1:T(8,128)S(1)}, u32[]{:S(2)}) copy-start(f32[3,2,729,16]{2,3,0,1:T(8,128)S(1)} %fusion.86) | copy-start | bytes 839812
  109.1 57.2 %copy-start.21 = (bf16[2,576,16]{1,2,0:T(8,128)(2,1)S(1)}, bf16[2,576,16]{1,2,0:T(8,128)(2,1)}, u32[]{:S(2)}) copy-start(bf16[2,576,16]{1,2,0:T(8,128)(2,1)} %gather_fusion.3) | copy-start | bytes 110596
  178.4 126.8 %all-gather.23.cloned.1.call-start = ((), (), s32[]{:S(2)}) async-start(), calls=%async_computation.12 | async-start | bytes 8478720 | tf_op jit(solution)/shard_map/all_gather | solution.py:224
  181.8 163.1 %all-gather.21.cloned.1.call-start = ((), (), s32[]{:S(2)}) async-start(), calls=%async_computation.10 | async-start | bytes 3317760 | tf_op jit(solution)/shard_map/all_gather | solution.py:125
  182.4 204.0 %all-gather.19.cloned.1.call-start = ((), (), s32[]{:S(2)}) async-start(), calls=%async_computation.9 | async-start | bytes 3317760 | tf_op jit(solution)/shard_map/all_gather | solution.py:124
  182.9 328.3 %all-gather.17.cloned.1.call-start = ((), (), s32[]{:S(2)}) async-start(), calls=%async_computation.8 | async-start | bytes 8478720 | tf_op jit(solution)/shard_map/all_gather | solution.py:190
  196.7 500.0 %reduce-scatter.9.cloned.1.call-start = ((), (), s32[]{:S(2)}) async-start(), calls=%async_computation.13 | async-start | bytes 8478720 | tf_op jit(solution)/shard_map/reduce_scatter | solution.py:244
  310.0 49.4 %copy-start.14 = (bf16[1,729,1152]{2,1,0:T(8,128)(2,1)S(1)}, bf16[1,729,1152]{2,1,0:T(8,128)(2,1)}, u32[]{:S(2)}) copy-start(bf16[1,729,1152]{2,1,0:T(8,128)(2,1)} %add_convert_fusion.4) | copy-start | bytes 5038852
  373.3 150.3 %copy-start.34 = (bf16[4,729,16]{1,2,0:T(8,128)(2,1)}, bf16[4,729,16]{1,2,0:T(8,128)(2,1)S(1)}, u32[]{:S(2)}) copy-start(bf16[4,729,16]{1,2,0:T(8,128)(2,1)S(1)} %all-gather.1) | copy-start | bytes 279940
  579.8 238.6 %reduce-scatter.7.cloned.1.call-start = ((), (), s32[]{:S(2)}) async-start(), calls=%async_computation.11 | async-start | bytes 8478720 | tf_op jit(solution)/shard_map/reduce_scatter | solution.py:219
  605.9 245.4 %all-gather.25.cloned.1.call-start = ((), (), s32[]{:S(2)}) async-start(), calls=%async_computation.14 | async-start | bytes 5087232 | tf_op jit(solution)/shard_map/all_gather | solution.py:263
  696.8 121.6 %copy-start.18 = (bf16[1,729,1152]{2,1,0:T(8,128)(2,1)S(1)}, bf16[1,729,1152]{2,1,0:T(8,128)(2,1)}, u32[]{:S(2)}) copy-start(bf16[1,729,1152]{2,1,0:T(8,128)(2,1)} %reduce-scatter.9.cloned.1.call-done) | copy-start | bytes 5038852
  824.8 175.7 %all-reduce.11.cloned.1.call-start = ((), (), s32[]{:S(2)}) async-start(), calls=%async_computation.18 | async-start | bytes 1179648 | tf_op jit(solution)/shard_map/psum | solution.py:327
  851.2 236.6 %all-reduce.9.cloned.1.call-start = ((), (), s32[]{:S(2)}) async-start(), calls=%async_computation.17 | async-start | bytes 2621440 | tf_op jit(solution)/shard_map/psum | solution.py:323
  863.4 99.9 %copy-start.26 = (f32[3,2,729,16]{2,3,0,1:T(8,128)S(1)}, f32[3,2,729,16]{2,3,0,1:T(8,128)}, u32[]{:S(2)}) copy-start(f32[3,2,729,16]{2,3,0,1:T(8,128)} %copy-done.25) | copy-start | bytes 839812
  972.4 262.2 %all-reduce.7.cloned.1.call-start = ((), (), s32[]{:S(2)}) async-start(), calls=%async_computation.16 | async-start | bytes 7077888 | tf_op jit(solution)/shard_map/psum | solution.py:319
  983.7 263.7 %reduce-scatter.11.cloned.1.call-start = ((), (), s32[]{:S(2)}) async-start(), calls=%async_computation.15 | async-start | bytes 5087232 | tf_op jit(solution)/shard_map/reduce_scatter | solution.py:294
  (68 other events, 420.4 us)
Sparse Core Ops, SparseCore 0:
  18.0 15.1 all-gather.10
  35.0 55.7 all-gather.12
  92.7 30.1 all-gather.14
  178.5 11.2 reduce-scatter.4
  824.9 12.9 all-gather.24
  851.3 55.7 all-reduce.10
  972.6 115.1 all-reduce.8
  1094.9 139.7 all-reduce.6
  1237.0 10.2 reduce-scatter.10
Sparse Core Ops, SparseCore 1:
  181.9 123.2 all-gather.22
  306.9 37.9 all-gather.20
  346.6 39.7 all-gather.18
  387.9 123.2 all-gather.16
  579.9 116.8 reduce-scatter.8
  699.2 119.1 reduce-scatter.6
where the time goes:
time: 1270 us
  waiting for transfers between devices  781 us (61%)
  matrix products  326 us (26%)
  other arithmetic  77 us (6%)
  local copies, waits for them, and re-layouts  49.9 us (4%)
  between operations  18.4 us (1%)
  blocking collectives  13.4 us (1%)
    psum x1, waiting for transfers between devices, per_device(): lax.psum((grad_qkv_in_part, grad_proj_out_part, grad_up_in_part, grad_dow...  143 us
    all_gather x1, waiting for transfers between devices, per_device(): lax.all_gather(second_norm_reduced, 'tensor', axis=0, tiled=True)  125 us
    reduce_scatter x1, waiting for transfers between devices, per_device(): lax.psum_scatter(mlp_part.astype(jnp.bfloat16), 'tensor', scatter_dimensi...  118 us
    all_gather x1, waiting for transfers between devices, per_device(): grad_mlp_in = lax.all_gather(grad_mlp, 'tensor', axis=0, tiled=True)  103 us
    reduce_scatter x1, waiting for transfers between devices, per_device(): lax.psum_scatter(grad_ln2.astype(jnp.bfloat16), 'tensor', scatter_dimensi...  90.2 us
    psum x1, waiting for transfers between devices, per_device(): lax.psum((grad_qkv_out_part, grad_proj_in_part), ('fsdp', 'tensor'))  76.5 us
    all_gather x1, waiting for transfers between devices, per_device(): lax.all_gather(query_key_value_weight, 'fsdp', axis=0, tiled=True)  54.6 us
    unnamed x129, local copies, waits for them, and re-layouts  35.5 us
  transfers between devices with their start and end apart: 15, of which 12 were waited for; matrix products, arithmetic and copies ran while one was open for 27% of the time, Pallas kernels for 0%

commit v1 on v0

v1 whole, which is shorter than its diff:
```python
import functools
import jax
import jax.numpy as jnp
from jax import lax
from jax.experimental import pallas as pl
from jax.experimental.pallas import tpu as pltpu
from jax.sharding import PartitionSpec as P

HEAD_DIM = 72
norm_eps = 1e-06
f32 = jnp.float32
bf16 = jnp.bfloat16
MESH = pl.DeviceIdType.MESH


def bits_of(n):
    return n.bit_length() - 1


class Comm:
    def __init__(self, send, recv):
        self.send, self.recv, self.n = send, recv, 0

    def new(self):
        self.n += 1
        return self.n - 1

    def copy(self, i, src, dst, **where):
        return pltpu.make_async_remote_copy(
            src_ref=src,
            dst_ref=dst,
            send_sem=self.send.at[i],
            recv_sem=self.recv.at[i],
            device_id=where,
            device_id_type=MESH,
        )


def enter(axes_sizes, f, h, z):
    fn, hn, tn = axes_sizes
    barrier = pltpu.get_barrier_semaphore()
    count = 0
    for b in range(bits_of(fn)):
        pl.semaphore_signal(
            barrier, 1, device_id={"fsdp": f ^ (1 << b)}, device_id_type=MESH
        )
        count += 1
    pl.semaphore_signal(barrier, 1, device_id={"heads": 1 - h}, device_id_type=MESH)
    count += 1
    for d in range(1, tn):
        pl.semaphore_signal(
            barrier, 1, device_id={"tensor": lax.rem(z + d, tn)}, device_id_type=MESH
        )
        count += 1
    pl.semaphore_wait(barrier, count)


class Rows:
    def __init__(self, comm, fn, f, slot, rows, own):
        self.comm, self.fn, self.f, self.slot, self.own = comm, fn, f, slot, own
        self.nb = bits_of(fn)
        half = rows // 2 // 8 * 8
        self.parts = ((0, half, list(range(self.nb))), (half, rows - half, list(range(self.nb))[::-1]))
        self.first = [comm.new() for _ in range(self.nb)]
        self.later = {}
        for p, (_, _, order) in enumerate(self.parts):
            for m in range(1, fn):
                last = max(order.index(b) for b in range(self.nb) if m >> b & 1)
                for b in order[last + 1 :]:
                    self.later[p, m, b] = comm.new()
        self.sent = []

    def part(self, origin, p):
        start, size, _ = self.parts[p]
        return self.slot(origin, pl.ds(start, size))

    def begin(self):
        for b in range(self.nb):
            c = self.comm.copy(
                self.first[b], self.own, self.slot(self.f, None), fsdp=self.f ^ (1 << b)
            )
            c.start()
            self.sent.append(c)

    def _arrived(self, m, p):
        order = self.parts[p][2]
        last = max(order.index(b) for b in range(self.nb) if m >> b & 1)
        b = order[last]
        src = m ^ (1 << b)
        if src == 0:
            return None
        where = self.part(self.f ^ m, p)
        return self.comm.copy(self.later[p, src, b], where, where, fsdp=self.f ^ (1 << b))

    def forward(self, m):
        if m & (m - 1) == 0:
            b = bits_of(m)
            where = self.slot(self.f ^ m, None)
            self.comm.copy(self.first[b], where, where, fsdp=self.f ^ m).wait_recv()
        for p, (_, _, order) in enumerate(self.parts):
            if m & (m - 1):
                self._arrived(m, p).wait_recv()
            last = max(order.index(b) for b in range(self.nb) if m >> b & 1)
            for b in order[last + 1 :]:
                where = self.part(self.f ^ m, p)
                c = self.comm.copy(self.later[p, m, b], where, where, fsdp=self.f ^ (1 << b))
                c.start()
                self.sent.append(c)

    def masks(self):
        return sorted(range(1, self.fn), key=lambda m: (bin(m).count("1"), m))

    def drain(self):
        for c in self.sent:
            c.wait_send()


def gather_kernel(
    sizes, wq, wo, w2, aq, ap, au, ad, oq, oo, o2, oaq, oap, oau, oad, send, recv, local
):
    fn, hn, tn = sizes
    f, h, z = lax.axis_index("fsdp"), lax.axis_index("heads"), lax.axis_index("tensor")
    rows = wo.shape[0]
    comm = Comm(send, recv)
    nothing = slice(None)

    def rs(r):
        return nothing if r is None else r

    jobq = Rows(comm, fn, f, lambda o, r: oq.at[:, h, o, rs(r)], rows, wq)
    jobo = Rows(comm, fn, f, lambda o, r: oo.at[h, o, rs(r)], rows, wo)
    blocks = [lax.rem(z + s, tn) for s in range(tn)]
    job2 = []
    for s in range(tn):
        own = w2.at[h] if s == 0 else o2.at[h, blocks[s], f]
        job2.append(
            Rows(comm, fn, f, lambda o, r, s=s: o2.at[h, blocks[s], o, rs(r)], rows, own)
        )
    up = [comm.new() for _ in range(tn - 1)]
    down = [comm.new() for _ in range(tn - 1)]
    sib = [comm.new() for _ in range(4 + tn)]
    small = [comm.new() for _ in range(2 * (tn - 1))]
    enter(sizes, f, h, z)

    locals_ = [
        pltpu.make_async_copy(wq, oq.at[:, h, f], local.at[0]),
        pltpu.make_async_copy(wo, oo.at[h, f], local.at[1]),
        pltpu.make_async_copy(w2.at[h], o2.at[h, z, f], local.at[2]),
        pltpu.make_async_copy(aq.at[h], oaq.at[h], local.at[3]),
        pltpu.make_async_copy(ap.at[h], oap.at[h], local.at[4]),
        pltpu.make_async_copy(au.at[z], oau.at[z], local.at[5]),
        pltpu.make_async_copy(ad.at[z], oad.at[z], local.at[6]),
    ]
    jobq.begin()
    jobo.begin()

    def zcopy(sem, k, block, src, to):
        return comm.copy(sem, src, o2.at[h, block, f], tensor=to)

    @pl.when(z < tn - 1)
    def _():
        zcopy(up[0], 0, z, w2.at[h], z + 1).start()

    @pl.when(z > 0)
    def _():
        zcopy(down[0], 0, z, w2.at[h], z - 1).start()

    for c in locals_:
        c.start()
    other = []
    for d in range(1, tn):
        p = lax.rem(z + d, tn)
        other.append(comm.copy(small[2 * d - 2], au.at[p], oau.at[z], tensor=p))
        other.append(comm.copy(small[2 * d - 1], ad.at[p], oad.at[z], tensor=p))
    other.append(comm.copy(sib[0], aq.at[1 - h], oaq.at[h], heads=1 - h))
    other.append(comm.copy(sib[1], ap.at[1 - h], oap.at[h], heads=1 - h))
    for c in other:
        c.start()
    job2[0].begin()
    for m in jobq.masks():
        jobq.forward(m)
        jobo.forward(m)
    locals_[0].wait()
    locals_[1].wait()
    sibq = comm.copy(sib[2], oq.at[:, h], oq.at[:, h], heads=1 - h)
    sibq.start()
    sibo = comm.copy(sib[3], oo.at[h], oo.at[h], heads=1 - h)
    sibo.start()
    for k in range(tn - 1):
        @pl.when(z - 1 - k >= 0)
        def _():
            b = o2.at[h, z - 1 - k, f]
            comm.copy(up[k], b, b, tensor=z - 1).wait_recv()
            if k + 1 < tn - 1:

                @pl.when(z < tn - 1)
                def _():
                    zcopy(up[k + 1], k, z - 1 - k, b, z + 1).start()

        @pl.when(z + 1 + k < tn)
        def _():
            b = o2.at[h, z + 1 + k, f]
            comm.copy(down[k], b, b, tensor=z + 1).wait_recv()
            if k + 1 < tn - 1:

                @pl.when(z > 0)
                def _():
                    zcopy(down[k + 1], k, z + 1 + k, b, z - 1).start()

    for s in range(1, tn):
        job2[s].begin()
    locals_[2].wait()
    sib2 = []
    for s in range(tn):
        for m in job2[s].masks():
            job2[s].forward(m)
        c = comm.copy(
            sib[4 + s], o2.at[h, blocks[s]], o2.at[h, blocks[s]], heads=1 - h
        )
        c.start()
        sib2.append(c)
    for c in locals_[3:]:
        c.wait()
    for k in range(tn - 1):

        @pl.when((z < tn - 1) & (z - k >= 0))
        def _():
            zcopy(up[k], k, z, w2.at[h], z + 1).wait_send()

        @pl.when((z > 0) & (z + k < tn))
        def _():
            zcopy(down[k], k, z, w2.at[h], z - 1).wait_send()

    for j in [jobq, jobo] + job2:
        j.drain()
    for c in other + [sibq, sibo] + sib2:
        c.wait_send()
    for d in range(1, tn):
        p = lax.rem(z + tn - d, tn)
        comm.copy(small[2 * d - 2], au.at[p], oau.at[p], tensor=p).wait_recv()
        comm.copy(small[2 * d - 1], ad.at[p], oad.at[p], tensor=p).wait_recv()
    comm.copy(sib[0], aq.at[h], oaq.at[1 - h], heads=1 - h).wait_recv()
    comm.copy(sib[1], ap.at[h], oap.at[1 - h], heads=1 - h).wait_recv()
    comm.copy(sib[2], oq.at[:, h], oq.at[:, 1 - h], heads=1 - h).wait_recv()
    comm.copy(sib[3], oo.at[h], oo.at[1 - h], heads=1 - h).wait_recv()
    for s in range(tn):
        b = o2.at[1 - h, blocks[s]]
        comm.copy(sib[4 + s], b, b, heads=1 - h).wait_recv()


def gather(sizes, wq, wo, w2, aq, ap, au, ad):
    fn, hn, tn = sizes
    rows, half = wo.shape
    units = w2.shape[-1]
    any_ = pl.BlockSpec(memory_space=pl.ANY)
    rank = au.shape[1]
    nb = bits_of(fn)
    nsem = (2 + tn) * (nb + 2 * (fn - 1 - nb)) + 4 * (tn - 1) + 4 + tn
    return pl.pallas_call(
        functools.partial(gather_kernel, sizes),
        out_shape=(
            jax.ShapeDtypeStruct((3, hn, fn, rows, half), bf16),
            jax.ShapeDtypeStruct((hn, fn, rows, half), bf16),
            jax.ShapeDtypeStruct((2, tn, fn, rows, units), bf16),
            jax.ShapeDtypeStruct((hn, 3, rank, half), bf16),
            jax.ShapeDtypeStruct((hn, rank, half), bf16),
            jax.ShapeDtypeStruct((tn, rank, units), bf16),
            jax.ShapeDtypeStruct((tn, rank, units), bf16),
        ),
        in_specs=[any_] * 7,
        out_specs=(any_,) * 7,
        scratch_shapes=[
            pltpu.SemaphoreType.DMA((nsem,)),
            pltpu.SemaphoreType.DMA((nsem,)),
            pltpu.SemaphoreType.DMA((7,)),
        ],
        compiler_params=pltpu.CompilerParams(collective_id=0, has_side_effects=True),
        name="gather_weights",
    )(wq, wo, w2, aq, ap, au, ad)


def normalize(values, gain, bias):
    mean = jnp.mean(values, axis=-1, keepdims=True)
    centred = values - mean
    inverse = lax.rsqrt(jnp.mean(centred * centred, axis=-1, keepdims=True) + norm_eps)
    unit = centred * inverse
    return (unit * gain + bias, unit, inverse)


def normalize_back(grad_norm, unit, inverse, gain):
    scaled = grad_norm * gain
    return inverse * (
        scaled
        - jnp.mean(scaled, axis=-1, keepdims=True)
        - unit * jnp.mean(scaled * unit, axis=-1, keepdims=True)
    )


def dot(a, b, dims):
    return lax.dot_general(a, b, (dims, ((), ())), preferred_element_type=f32)


def mm(a, b):
    return dot(a, b, ((1,), (0,)))


def mmt(a, b):
    return dot(a, b, ((1,), (1,)))


def tmm(a, b):
    return dot(a, b, ((0,), (0,)))


def attend_forward(query, keyed, valued):
    scores = jnp.einsum("qhd,khd->hqk", query, keyed, preferred_element_type=f32) * HEAD_DIM ** (-0.5)
    top = jnp.max(scores, axis=-1, keepdims=True)
    weights = jnp.exp(scores - top)
    total = jnp.sum(weights, axis=-1, keepdims=True)
    probs = (weights / total).astype(bf16)
    mixed = jnp.einsum("hqk,khd->qhd", probs, valued, preferred_element_type=f32)
    return mixed.astype(bf16), (top + jnp.log(total))[..., 0]


def attend_back(query, keyed, valued, grad_mixed, log_total):
    scale = HEAD_DIM ** (-0.5)
    scores = jnp.einsum("qhd,khd->hqk", query, keyed, preferred_element_type=f32) * scale
    probs = jnp.exp(scores - log_total[..., None])
    grad_probs = jnp.einsum("qhd,khd->hqk", grad_mixed, valued, preferred_element_type=f32)
    grad_values = jnp.einsum("hqk,qhd->khd", probs.astype(bf16), grad_mixed, preferred_element_type=f32)
    inner = jnp.sum(probs * grad_probs, axis=-1, keepdims=True)
    grad_scores = (probs * (grad_probs - inner)).astype(bf16)
    grad_query = jnp.einsum("hqk,khd->qhd", grad_scores, keyed, preferred_element_type=f32) * scale
    grad_keys = jnp.einsum("hqk,qhd->khd", grad_scores, query, preferred_element_type=f32) * scale
    return grad_query, grad_keys, grad_values


def per_device(
    inputs,
    cotangent,
    image_adapter_index,
    first_norm_gain,
    first_norm_bias,
    second_norm_gain,
    second_norm_bias,
    query_key_value_weight,
    attention_output_weight,
    up_weight,
    down_weight,
    up_projection_bias,
    down_projection_bias,
    query_key_value_adapter_first,
    query_key_value_adapter_second,
    projection_adapter_first,
    projection_adapter_second,
    up_adapter_first,
    up_adapter_second,
    down_adapter_first,
    down_adapter_second,
):
    sizes = tuple(lax.axis_size(a) for a in ("fsdp", "heads", "tensor"))
    fn, hn, tn = sizes
    f, h, z = (lax.axis_index(a) for a in ("fsdp", "heads", "tensor"))
    images, length, width = inputs.shape
    assert images == 1
    heads_n = width // HEAD_DIM
    count = query_key_value_adapter_first.shape[1]
    own = (f * hn + h) * tn + z
    number = image_adapter_index[own]
    pair = image_adapter_index[(f * hn + jnp.arange(hn)) * tn + z]
    line = image_adapter_index[(f * hn + h) * tn + jnp.arange(tn)]
    aq = jnp.swapaxes(query_key_value_adapter_second[:, pair], 0, 1)
    ap = jnp.swapaxes(projection_adapter_first, 1, 2)[pair]
    au, ad = up_adapter_second[line], down_adapter_first[line]
    wq, wo, w2, aq, ap, au, ad = gather(
        sizes,
        jnp.swapaxes(query_key_value_weight, 0, 1),
        attention_output_weight,
        jnp.stack([up_weight, down_weight]),
        aq,
        ap,
        au,
        ad,
    )
    wq = jnp.moveaxis(wq.reshape(3, hn, width, width // hn), 1, 2).reshape(3, width, width)
    wo = jnp.moveaxis(wo.reshape(hn, width, width // hn), 0, 1).reshape(width, width)
    wu, wd = w2[0].reshape(tn, width, -1), w2[1].reshape(tn, width, -1)
    qkv_in = jnp.swapaxes(query_key_value_adapter_first[:, number], 1, 2)
    qkv_out = jnp.moveaxis(aq, 0, 2).reshape(3, -1, width)
    p_in = jnp.moveaxis(ap, 0, 1).reshape(-1, width)
    p_out = projection_adapter_second[number]
    u_in = up_adapter_first[number].T
    d_out = down_adapter_second[number]
    b_up = up_projection_bias
    b_up = lax.all_gather(b_up, "tensor").astype(f32)

    x, g = inputs[0], cotangent[0]
    n1, unit1, inv1 = normalize(x, first_norm_gain, first_norm_bias)
    ln1 = n1.astype(bf16)
    qkv_mid = jnp.stack([mmt(ln1, qkv_in[j]) for j in range(3)]).astype(bf16)
    proj = [(mm(ln1, wq[j]) + mm(qkv_mid[j], qkv_out[j])).astype(bf16) for j in range(3)]
    shaped = [p.reshape(length, heads_n, HEAD_DIM) for p in proj]
    mixed, log_total = attend_forward(*shaped)
    mixed = mixed.reshape(length, width)
    proj_mid = mmt(mixed, p_in).astype(bf16)
    hidden = x + mmt(mixed, wo) + mm(proj_mid, p_out)
    n2, unit2, inv2 = normalize(hidden, second_norm_gain, second_norm_bias)
    ln2 = n2.astype(bf16)
    up_mid = mmt(ln2, u_in).astype(bf16)
    g_mlp = g.astype(bf16)
    g_down_mid = mmt(g_mlp, d_out).astype(bf16)
    out, g_ln2, down_mid, g_up_mid = 0.0, 0.0, 0.0, 0.0
    g_up_out, g_down_in, kept = [], [], []
    for t in range(tn):
        before = mm(ln2, wu[t]) + mm(up_mid, au[t]) + b_up[t]
        act, pull = jax.vjp(lambda v: jax.nn.gelu(v, approximate=True), before)
        act = act.astype(bf16)
        g_act = mm(g_mlp, wd[t]) + mm(g_down_mid, ad[t])
        g_before = pull(g_act)[0].astype(bf16)
        out += mmt(act, wd[t])
        g_ln2 += mmt(g_before, wu[t])
        down_mid += mmt(act, ad[t])
        g_up_mid += mmt(g_before, au[t])
        g_up_out.append(tmm(up_mid, g_before))
        g_down_in.append(tmm(g_down_mid, act))
    down_mid, g_up_mid = down_mid.astype(bf16), g_up_mid.astype(bf16)
    layer_output = hidden + out + mm(down_mid, d_out) + down_projection_bias.astype(f32)
    g_ln2 += mm(g_up_mid, u_in)
    g_hidden = g + normalize_back(g_ln2, unit2, inv2, second_norm_gain)
    g_branch = g_hidden.astype(bf16)
    g_proj_mid = mmt(g_branch, p_out).astype(bf16)
    g_mixed = (mm(g_branch, wo) + mm(g_proj_mid, p_in)).astype(bf16)
    g3 = attend_back(*shaped, g_mixed.reshape(length, heads_n, HEAD_DIM), log_total)
    g_proj = [v.reshape(length, width).astype(bf16) for v in g3]
    g_qkv_mid = [mmt(g_proj[j], qkv_out[j]).astype(bf16) for j in range(3)]
    g_ln1 = sum(mmt(g_proj[j], wq[j]) + mm(g_qkv_mid[j], qkv_in[j]) for j in range(3))
    grad_input = g_hidden + normalize_back(g_ln1, unit1, inv1, first_norm_gain)

    hot = (jnp.arange(count) == number).astype(f32)

    def spread(v):
        return (hot.reshape((count,) + (1,) * v.ndim) * v[None]).astype(bf16)

    everyone = ("fsdp", "heads", "tensor")
    s1 = jnp.concatenate(
        [tmm(g_qkv_mid[j], ln1) for j in range(3)]
        + [tmm(proj_mid, g_branch), tmm(g_up_mid, ln2), tmm(down_mid, g_mlp)]
        + [tmm(qkv_mid[j], g_proj[j]) for j in range(3)]
        + [tmm(g_proj_mid, mixed)]
    )
    s1 = lax.psum(spread(s1), everyone).astype(f32)
    s3 = lax.psum(spread(jnp.stack([jnp.concatenate(g_up_out, 1), jnp.concatenate(g_down_in, 1)])), everyone)
    s3 = s3.astype(f32).reshape(count, 2, -1, tn, wu.shape[-1])[:, :, :, z]
    r = s1.shape[1] // 10

    def rows(i, k=1):
        return s1[:, i * r : (i + k) * r]

    def own_half(v):
        return lax.dynamic_slice_in_dim(v, h * (width // hn), width // hn, axis=-1)

    def three(v):
        return jnp.swapaxes(v.reshape(count, 3, r, -1), 0, 1)

    return (
        layer_output[None],
        grad_input[None],
        jnp.swapaxes(three(rows(0, 3)), 2, 3),
        own_half(three(rows(6, 3))),
        jnp.swapaxes(own_half(rows(9)), 1, 2),
        rows(3),
        jnp.swapaxes(rows(4), 1, 2),
        s3[:, 0],
        s3[:, 1],
        rows(5),
    )

def solution(mesh):
    in_specs = (
        P(("fsdp", "heads", "tensor"), None, None),
        P(("fsdp", "heads", "tensor"), None, None),
        P(),
        P(),
        P(),
        P(),
        P(),
        P("fsdp", None, "heads"),
        P("fsdp", "heads"),
        P("fsdp", "tensor"),
        P("fsdp", "tensor"),
        P("tensor"),
        P(),
        P(),
        P(None, None, None, "heads"),
        P(None, "heads", None),
        P(),
        P(),
        P(None, None, "tensor"),
        P(None, None, "tensor"),
        P(),
    )
    out_specs = (
        P(("fsdp", "heads", "tensor"), None, None),
        P(("fsdp", "heads", "tensor"), None, None),
        P(),
        P(None, None, None, "heads"),
        P(None, "heads", None),
        P(),
        P(),
        P(None, None, "tensor"),
        P(None, None, "tensor"),
        P(),
    )
    return jax.shard_map(
        per_device, mesh=mesh, in_specs=in_specs, out_specs=out_specs, check_vma=False
    )
```

time: 1270 us -> 751 us (0.59)
  waiting for transfers between devices: 781 us -> 119 us
  Pallas kernels: 0 us -> 170 us
  matrix products: 326 us -> 244 us
  local copies, waits for them, and re-layouts: 49.9 us -> 95.9 us
    all_gather x8 -> x0, waiting for transfers between devices: 337 us -> none  [the longest x1 125 us: per_device(): lax.all_gather(second_norm_reduced, 'tensor', axis=0, tiled=True)]
    reduce_scatter x4 -> x0, waiting for transfers between devices: 222 us -> none  [the longest x1 118 us: per_device(): lax.psum_scatter(mlp_part.astype(jnp.bfloat16), 'tensor', scatter_dimensi...]
    pallas_call x0 -> x1, Pallas kernels: none -> 170 us  [gather(): pl.pallas_call(functools.partial(gather_kernel, sizes), out_shape=(jax.Sh...]
    psum x3 -> x1, waiting for transfers between devices: 219 us -> 119 us  [per_device(): s1 = lax.psum(spread(s1), everyone).astype(f32)]
    dot_general x54 -> x84, matrix products: 326 us -> 244 us  [the longest x78 150 us: dot(): return lax.dot_general(a, b, (dims, ((), ())), preferred_element_type=f32)]
    reshape x0 -> x5, local copies, waits for them, and re-layouts: none -> 23.4 us  [the longest x1 12.5 us: per_device(): wq.reshape(3, hn, width, width // hn)]
    slice x1 -> x9, local copies, waits for them, and re-layouts: 2.13 us -> 23.1 us  [the longest x1 14.1 us: per_device(): out += mmt(act, wd[t])]
    unnamed x0 -> x1, blocking collectives: none -> 20.7 us
  transfers between devices with their start and end apart: 15 -> 1, of which waited for: 12 -> 1; matrix products, arithmetic and copies ran while one was open for 27% -> 4% of each run, Pallas kernels for 0% -> 0%
where the time goes in v1:
time: 751 us; the launch traced here: 745 us
  matrix products  244 us (32%)
  Pallas kernels  170 us (23%)
  waiting for transfers between devices  119 us (16%)
  local copies, waits for them, and re-layouts  95.9 us (13%)
  other arithmetic  76.9 us (10%)
  blocking collectives  20.7 us (3%)
  between operations  18.5 us (2%)
    pallas_call x1, Pallas kernels, gather(): pl.pallas_call(functools.partial(gather_kernel, sizes), out_shape=(jax.Sh...  170 us
    dot_general x78, matrix products, dot(): return lax.dot_general(a, b, (dims, ((), ())), preferred_element_type=f32)  150 us
    psum x1, waiting for transfers between devices, per_device(): s1 = lax.psum(spread(s1), everyone).astype(f32)  119 us
    convert_element_type x1, other arithmetic, attend_back(): grad_scores = (probs * (grad_probs - inner)).astype(bf16)  30.5 us
    dot_general x1, matrix products, attend_back(): jnp.einsum('qhd,khd->hqk', grad_mixed, valued, preferred_element_type=f32)  28.7 us
    unnamed x202, local copies, waits for them, and re-layouts  22.5 us
    unnamed x1, blocking collectives  20.7 us
    dot_general x1, matrix products, attend_forward(): jnp.einsum('hqk,khd->qhd', probs, valued, preferred_element_type=f32)  16.2 us
  transfers between devices with their start and end apart: 1, of which 1 were waited for; matrix products, arithmetic and copies ran while one was open for 4% of the time, Pallas kernels for 0%

profile of v1, /device:TPU:0, one launch (start us, length us, event | category | flops | bytes accessed | tf_op | source)
XLA Modules:
  0.0 744.7 jit_solution(11345121749852120540)
XLA Ops:
  18.9 5.6 add_convert_fusion.2
  30.4 20.7 %all-reduce = bf16[4304]{0:T(1024)(128)(2,1)S(1)} all-reduce(bf16[4304]{0:T(1024)(128)(2,1)S(1)} %dynamic-update-slice), channel_id=2, replica_groups=mesh['fsdp'=4,'heads'=2,'tensor'=4] {'tensor'}, use_global_device_ids=true, to_apply=%add | all-reduce | flops 4304 | bytes 17216
  65.6 169.8 %gather_weights.1 = (bf16[3,2,4,288,576]{4,3,2,1,0:T(8,128)(2,1)}, bf16[2,4,288,576]{3,2,1,0:T(8,128)(2,1)}, bf16[2,4,4,288,1076]{4,3,2,1,0:T(8,128)(2,1)}, bf16...) custom-call(bf16[3,288,576]{2,1,0:T(8,128)(2,1)} %bitcast.397, ...), custom_call_target="tpu_custom_call" | custom-call | tf_op jit(solution)/shard_map/gather_weights/pallas_call | solution.py:259
  235.4 12.5 %copy.65 = bf16[3,2,1152,576]{2,3,1,0:T(8,128)(2,1)} copy(bf16[3,2,1152,576]{3,2,1,0:T(8,128)(2,1)} %bitcast.368) | data formatting | bytes 15925248 | tf_op jit(solution)/shard_map/reshape | solution.py:385
  248.1 5.6 fusion.152
  267.6 5.5 fusion.63
  279.0 4.9 fusion.71
  289.6 14.1 %fusion.151 = (bf16[1,1,4,288,1076]{4,3,2,1,0:T(8,128)(2,1)}, bf16[1,1,4,288,1076]{4,3,2,1,0:T(8,128)(2,1)}, bf16[1,1,4,288,1076]{4,3,2,1,0:T(8,128)(2,1)}, bf16...) fusion(bf16[2,4,4,288,1076]{4,3,2,1,0:T(8,128)(2,1)} %get-tuple, ...), kind=kLoop, calls=%fused_computation.264 | loop fusion | bytes 39665664 | tf_op jit(solution)/shard_map/slice | solution.py:420
  309.2 14.2 %multiply_reduce_fusion.1 = (f32[16,729]{1,0:T(8,128)S(1)}, f32[16,729,729]{1,2,0:T(8,128)}) fusion(bf16[729,16,72]{0,2,1:T(8,128)(2,1)S(1)} %bitcast.347, bf16[729,16,72]{0,2,1:T(8,128)(2,1)S(1)} %bitcast.353), kind=kOutput, calls=%fused_computation.12 | convolution fusion | flops 1241434496 | bytes 37418112 | tf_op jit(solution)/shard_map/qhd,khd->hqk/dot_general | solution.py:316
  323.4 15.5 %fusion = f32[16,729]{1,0:T(8,128)S(1)} fusion(f32[16,729,729]{1,2,0:T(8,128)} %get-tuple-element.88, f32[16,729]{1,0:T(8,128)S(1)} %get-tuple-element.87), kind=kLoop, calls=%fused_computation.11 | loop fusion | flops 25497504 | bytes 34105536 | tf_op jit(solution)/shard_map/reduce_sum | solution.py:319
  339.6 16.2 %fusion.51 = bf16[16,72,729]{2,1,0:T(8,128)(2,1)} fusion(bf16[729,16,72]{0,2,1:T(8,128)(2,1)S(1)} %bitcast.361, f32[16,729,729]{1,2,0:T(8,128)} %get-tuple-element.88, f32[16,729]{1,0:T(8,128)S(1)} %fusion, f32[16,729]{1,0:T(8,128)S(1)} %get-tuple-element.87), kind=kOutput, calls=%fused_computation.130 | convolution fusion | flops 1259292032 | bytes 37464768 | tf_op jit(solution)/shard_map/hqk,khd->qhd/dot_general | solution.py:321
  357.6 6.0 convolution_add_fusion.24
  438.3 15.0 %fusion.52 = bf16[16,72,729]{2,1,0:T(8,128)(2,1)S(1)} fusion(bf16[729,16,72]{0,2,1:T(8,128)(2,1)} %bitcast.358, f32[16,729,729]{1,2,0:T(8,128)} %get-tuple-element.88, f32[16,729]{1,0:T(8,128)S(1)} %copy-done.49), kind=kOutput, calls=%fused_computation.131 | convolution fusion | flops 1250788992 | bytes 37418112 | tf_op jit(solution)/shard_map/hqk,qhd->khd/dot_general | solution.py:330
  453.6 6.3 fusion.166
  460.0 28.7 %multiply_reduce_fusion = (f32[16,729]{1,0:T(8,128)S(1)}, f32[16,729,729]{1,2,0:T(8,128)}) fusion(f32[16,729,729]{1,2,0:T(8,128)} %get-tuple-element.88, f32[16,729]{1,0:T(8,128)S(1)} %copy-done.49, bf16[729,16,72]{0,2,1:T(8,128)(2,1)} %bitcast.359, bf16[729,16,72]{0,2,1:T(8,128)(2,1)} %bitcast.360), kind=kOutput, calls=%fused_computation.7 | convolution fusion | flops 1258440576 | bytes 71476992 | tf_op jit(solution)/shard_map/qhd,khd->hqk/dot_general | solution.py:329
  488.7 30.5 %multiply_convert_fusion = bf16[16,729,729]{1,2,0:T(8,128)(2,1)} fusion(f32[16,729,729]{1,2,0:T(8,128)} %get-tuple-element.101, f32[16,729,729]{1,2,0:T(8,128)} %get-tuple-element.88, f32[16,729]{1,0:T(8,128)S(1)} %get-tuple-element.100, f32[16,729]{1,0:T(8,128)S(1)} %copy-done.49), kind=kLoop, calls=%fused_computation.6 | loop fusion | flops 42515280 | bytes 85123872 | tf_op jit(solution)/shard_map/convert_element_type | solution.py:332
  519.1 10.0 %multiply_convert_fusion.3 = bf16[16,72,729]{2,1,0:T(8,128)(2,1)S(1)} fusion(bf16[729,16,72]{0,2,1:T(8,128)(2,1)} %bitcast.348, bf16[16,729,729]{1,2,0:T(8,128)(2,1)} %multiply_convert_fusion), kind=kOutput, calls=%fused_computation.68 | convolution fusion | flops 1226119680 | bytes 20365344 | tf_op jit(solution)/shard_map/hqk,qhd->khd/dot_general | solution.py:334
  529.1 9.5 %multiply_convert_fusion.4 = bf16[16,72,729]{2,1,0:T(8,128)(2,1)S(1)} fusion(bf16[729,16,72]{0,2,1:T(8,128)(2,1)S(1)} %bitcast.354, bf16[16,729,729]{1,2,0:T(8,128)(2,1)} %multiply_convert_fusion), kind=kOutput, calls=%fused_computation.69 | convolution fusion | flops 1226119680 | bytes 20365344 | tf_op jit(solution)/shard_map/hqk,khd->qhd/dot_general | solution.py:333
  553.2 4.8 reshape.406
  576.9 6.8 fusion.159
  583.7 5.6 convolution_add_fusion.23
  597.2 5.2 copy.81
  602.4 5.2 copy.82
  607.6 119.1 %all-reduce.4.cloned.1.call-done = (bf16[8,160,1152]{2,1,0:T(8,128)(2,1)}, bf16[8,2,16,4,1076]{4,3,2,1,0:T(4,128)(2,1)}) async-done(((bf16[8,160,1152]{2,1,0:T(8,128)(2,1)}, bf16[8,2,16,4,1076]{4,3,2,1,0:T(4,128)(2,1)}), (bf16[8,160,1152]{2,1,0:T(8,128)(2,1)}, bf16[8,2,16,4,1076]{4,3,2,1,0:T(4,128)(2,1)})) %all-reduce.4.cloned.1.call-update) | async-done | bytes 5152784 | tf_op jit(solution)/shard_map/psum | solution.py:451
  (337 shorter events, 189.2 us)
Async XLA Ops:
  7.2 18.5 %copy-start = (bf16[3,8,1152,16]{2,3,1,0:T(8,128)(2,1)S(1)}, bf16[3,8,1152,16]{2,3,1,0:T(8,128)(2,1)}, u32[]{:S(2)}) copy-start(bf16[3,8,1152,16]{2,3,1,0:T(8,128)(2,1)} %param.34) | copy-start | bytes 2654212
  7.2 719.5 %all-reduce.4.cloned.1.call-start = ((), (), s32[]{:S(2)}) async-start(), calls=%async_computation | async-start | bytes 10616832 | tf_op jit(solution)/shard_map/psum | solution.py:451
  11.1 7.9 %copy-start.78 = (f32[1152]{0:T(1024)S(1)}, f32[1152]{0:T(1024)}, u32[]{:S(2)}) copy-start(f32[1152]{0:T(1024)} %param.24) | copy-start | bytes 13828
  15.8 8.8 %copy-start.76 = (f32[729]{0:T(1024)}, f32[729]{0:T(1024)S(1)}, u32[]{:S(2)}) copy-start(f32[729]{0:T(1024)S(1)} %broadcast_multiply_fusion.5) | copy-start | bytes 8752
  24.8 234.0 %copy-start.16 = (bf16[1,729,1152]{2,1,0:T(8,128)(2,1)}, bf16[1,729,1152]{2,1,0:T(8,128)(2,1)S(1)}, u32[]{:S(2)}) copy-start(bf16[1,729,1152]{2,1,0:T(8,128)(2,1)S(1)} %copy.88) | copy-start | bytes 5038852
  25.7 30.4 %copy-start.80 = (bf16[8,16,1076]{2,1,0:T(8,128)(2,1)S(1)}, bf16[8,16,1076]{2,1,0:T(8,128)(2,1)}, u32[]{:S(2)}) copy-start(bf16[8,16,1076]{2,1,0:T(8,128)(2,1)} %param.40) | copy-start | bytes 826372
  25.7 31.6 %copy-start.81 = (bf16[8,16,1076]{2,1,0:T(8,128)(2,1)S(1)}, bf16[8,16,1076]{2,1,0:T(8,128)(2,1)}, u32[]{:S(2)}) copy-start(bf16[8,16,1076]{2,1,0:T(8,128)(2,1)} %param.39) | copy-start | bytes 826372
  26.3 257.7 %copy-start.66 = (bf16[729,16]{0,1:T(8,128)(2,1)}, bf16[729,16]{0,1:T(8,128)(2,1)S(1)}, u32[]{:S(2)}) copy-start(bf16[729,16]{0,1:T(8,128)(2,1)S(1)} %fusion.75) | copy-start | bytes 69988
  26.9 236.3 %copy-start.70 = (bf16[729,16]{0,1:T(8,128)(2,1)}, bf16[729,16]{0,1:T(8,128)(2,1)S(1)}, u32[]{:S(2)}) copy-start(bf16[729,16]{0,1:T(8,128)(2,1)S(1)} %fusion.78) | copy-start | bytes 69988
  27.4 245.7 %copy-start.68 = (bf16[729,16]{0,1:T(8,128)(2,1)}, bf16[729,16]{0,1:T(8,128)(2,1)S(1)}, u32[]{:S(2)}) copy-start(bf16[729,16]{0,1:T(8,128)(2,1)S(1)} %fusion.81) | copy-start | bytes 69988
  235.4 12.5 %copy-start.75 = (bf16[2,3,16,576]{3,2,1,0:T(8,128)(2,1)S(1)}, bf16[2,3,16,576]{3,2,1,0:T(8,128)(2,1)}, u32[]{:S(2)}) copy-start(bf16[2,3,16,576]{3,2,1,0:T(8,128)(2,1)} %get-tuple-element.18) | copy-start | bytes 331780
  248.1 25.1 %copy-start.55 = (bf16[16,1152]{1,0:T(8,128)(2,1)}, bf16[16,1152]{1,0:T(8,128)(2,1)S(1)}, u32[]{:S(2)}) copy-start(bf16[16,1152]{1,0:T(8,128)(2,1)S(1)} %squeeze.156) | copy-start | bytes 110596
  253.8 9.4 %copy-start.57 = (bf16[16,1152]{1,0:T(8,128)(2,1)}, bf16[16,1152]{1,0:T(8,128)(2,1)S(1)}, u32[]{:S(2)}) copy-start(bf16[16,1152]{1,0:T(8,128)(2,1)S(1)} %squeeze.152) | copy-start | bytes 110596
  254.0 30.0 %copy-start.59 = (bf16[16,1152]{1,0:T(8,128)(2,1)}, bf16[16,1152]{1,0:T(8,128)(2,1)S(1)}, u32[]{:S(2)}) copy-start(bf16[16,1152]{1,0:T(8,128)(2,1)S(1)} %squeeze.148) | copy-start | bytes 110596
  267.6 41.6 %copy-start.9 = (bf16[729,1152]{0,1:T(8,128)(2,1)}, bf16[729,1152]{0,1:T(8,128)(2,1)S(1)}, u32[]{:S(2)}) copy-start(bf16[729,1152]{0,1:T(8,128)(2,1)S(1)} %copy.69) | copy-start | bytes 5038852
  289.6 14.1 %copy-start.29 = (bf16[1,729,1152]{2,1,0:T(8,128)(2,1)S(1)}, bf16[1,729,1152]{2,1,0:T(8,128)(2,1)}, u32[]{:S(2)}) copy-start(bf16[1,729,1152]{2,1,0:T(8,128)(2,1)} %copy.90) | copy-start | bytes 5038852
  323.4 16.2 %copy-start.22 = (bf16[729,1152]{0,1:T(8,128)(2,1)S(1)}, bf16[729,1152]{0,1:T(8,128)(2,1)}, u32[]{:S(2)}) copy-start(bf16[729,1152]{0,1:T(8,128)(2,1)} %copy.67) | copy-start | bytes 5038852
  365.1 63.3 %copy-start.3 = (f32[729,1152]{1,0:T(8,128)}, f32[729,1152]{1,0:T(8,128)S(1)}, u32[]{:S(2)}) copy-start(f32[729,1152]{1,0:T(8,128)S(1)} %get-tuple-element.90) | copy-start | bytes 10077700
  366.4 41.7 %copy-start.20 = (bf16[729,1152]{1,0:T(8,128)(2,1)}, bf16[729,1152]{1,0:T(8,128)(2,1)S(1)}, u32[]{:S(2)}) copy-start(bf16[729,1152]{1,0:T(8,128)(2,1)S(1)} %add_convert_fusion.1) | copy-start | bytes 5038852
  373.1 8.8 %copy-start.37 = (bf16[729,1076]{0,1:T(8,128)(2,1)}, bf16[729,1076]{0,1:T(8,128)(2,1)S(1)}, u32[]{:S(2)}) copy-start(bf16[729,1076]{0,1:T(8,128)(2,1)S(1)} %get-tuple-element.91) | copy-start | bytes 4706428
  438.2 15.0 %copy-start.60 = (bf16[16,1152]{1,0:T(8,128)(2,1)S(1)}, bf16[16,1152]{1,0:T(8,128)(2,1)}, u32[]{:S(2)}) copy-start(bf16[16,1152]{1,0:T(8,128)(2,1)} %copy-done.59) | copy-start | bytes 110596
  519.1 10.0 %copy-start.13 = (bf16[729,1152]{0,1:T(8,128)(2,1)S(1)}, bf16[729,1152]{0,1:T(8,128)(2,1)}, u32[]{:S(2)}) copy-start(bf16[729,1152]{0,1:T(8,128)(2,1)} %copy.71) | copy-start | bytes 5038852
  529.1 9.5 %copy-start.56 = (bf16[16,1152]{1,0:T(8,128)(2,1)S(1)}, bf16[16,1152]{1,0:T(8,128)(2,1)}, u32[]{:S(2)}) copy-start(bf16[16,1152]{1,0:T(8,128)(2,1)} %copy-done.55) | copy-start | bytes 110596
  529.1 9.8 %copy-start.27 = (bf16[1,1152,2,576]{1,3,2,0:T(8,128)(2,1)S(1)}, bf16[1,1152,2,576]{1,3,2,0:T(8,128)(2,1)}, u32[]{:S(2)}) copy-start(bf16[1,1152,2,576]{1,3,2,0:T(8,128)(2,1)} %get-tuple-element.68) | copy-start | bytes 7962628
  (74 other events, 235.6 us)
Sparse Core Ops, SparseCore 0:
  577.0 149.6 all-reduce.3
